TPU v7x, 32 devices: a whole 2x2x4 slice. The times are simulated.
32 devices in a mesh: groups: 2 (over y), dp: 4 (over z), feat: 2 (over core), ens: 2 (over x).
Axes of the slice: x: 2, y: 2, z: 4, core: 2. Of those that a mesh axis runs over, the one named last changes fastest.
Arguments:
- test_feat: bfloat16 [2, 64, 8192], P('ens', 'groups', 'dp'), parts along dimension 1, may hold values from -6 to 6
- kernel_inverse: bfloat16 [2, 8192, 8192], P('ens', 'dp', 'feat'), may hold values from -0.0625 to 0.0625
- train_feat: bfloat16 [2, 1024, 8192], P('ens', 'dp', 'feat'), may hold values from -0.0625 to 0.0625
- residual_weight: float32 [2, 1024], P('ens', 'dp'), may hold values from 0.05 to 1
Outputs:
- scores: float32 [64, 1024], P(('groups', 'feat', 'ens'), 'dp'), parts along dimension 0
There are 2 independent parts, one for each index of `groups`. A program takes and returns all parts, laid end to end along the dimension named above; an argument that names none is the same for every part. Nothing has to cross between parts.
All inputs are finite; a program needn't handle non-finite values.
Results may differ from a plain program's by a relative error of at most 0.0029.
Values may be sent and summed in bfloat16 or wider, within the bound.
A program may use at most 64 MiB of HBM per device.

v0:
```python
import jax
import jax.numpy as jnp
from jax import lax
from jax.sharding import PartitionSpec as P


def shards(test_feat, kernel_inverse, train_feat, residual_weight):
    test_local = test_feat[0]
    inverse_local = kernel_inverse[0]
    train_local = train_feat[0]
    weight_row = residual_weight[0][None, :]
    partial_sum = jnp.dot(test_local, inverse_local, preferred_element_type=jnp.float32)
    projected = lax.psum(partial_sum, "dp").astype(jnp.bfloat16)
    raw = jnp.einsum("tf,nf->tn", projected, train_local, preferred_element_type=jnp.float32)
    totals = raw * weight_row
    return lax.psum_scatter(totals, ("feat", "ens"), scatter_dimension=0, tiled=True)


def solution(mesh):
    in_specs = (
        P("ens", "groups", "dp"),
        P("ens", "dp", "feat"),
        P("ens", "dp", "feat"),
        P("ens", "dp"),
    )
    out_specs = P(("groups", "feat", "ens"), "dp")
    return jax.shard_map(shards, mesh=mesh, in_specs=in_specs, out_specs=out_specs, check_vma=False)
```

profile of v0, /device:TPU:0, one launch (start us, length us, event | category | flops | bytes accessed | tf_op | source)
XLA Modules:
  0.0 74.1 jit_solution(5447746823196072305)
XLA Ops:
  6.5 0.0 copy-start
  6.5 0.0 copy-start.1
  6.5 0.0 reduce-scatter.2.cloned.1.call-start
  6.5 9.0 %fusion = f32[32,4096]{1,0:T(8,128)S(1)} fusion(bf16[1,2048,4096]{2,1,0:T(8,128)(2,1)} %param.5, bf16[1,32,2048]{2,1,0:T(8,128)(2,1)} %param.4), kind=kOutput, calls=%fused_computation | convolution fusion | flops 536870912 | bytes 17432576 | tf_op jit(solution)/shard_map/dot_general | solution.py:12
  15.5 32.1 %all-reduce.1 = bf16[32,4096]{1,0:T(8,128)(2,1)S(1)} all-reduce(f32[32,4096]{1,0:T(8,128)S(1)} %fusion), channel_id=1, replica_groups=mesh['groups'=2,'dp'=4,'feat'=2,'ens'=2] {'dp'}, use_global_device_ids=true, to_apply=%region_0.0 | all-reduce | flops 131072 | bytes 786432 | tf_op jit(solution)/shard_map/psum | solution.py:13
  47.6 0.0 copy-done
  47.6 0.0 copy-done.1
  47.6 1.3 %fusion.4 = f32[32,256]{1,0:T(8,128)} fusion(bf16[1,256,4096]{2,1,0:T(8,128)(2,1)S(1)} %copy-done, bf16[32,4096]{1,0:T(8,128)(2,1)S(1)} %all-reduce.1, f32[256]{0:T(256)S(1)} %bitcast.13), kind=kOutput, calls=%fused_computation.4 | convolution fusion | flops 67117056 | bytes 2393088 | tf_op jit(solution)/shard_map/tf,nf->tn/dot_general | solution.py:14
  49.0 0.0 reduce-scatter.2.cloned.1.call-update
  49.0 18.2 %reduce-scatter.2.cloned.1.call-done = f32[8,256]{1,0:T(8,128)} async-done(((f32[32,256]{1,0:T(8,128)}), f32[8,256]{1,0:T(8,128)}) %reduce-scatter.2.cloned.1.call-update) | async-done | bytes 8208 | tf_op jit(solution)/shard_map/reduce_scatter | solution.py:16
Async XLA Ops:
  6.5 41.1 %copy-start = (bf16[1,256,4096]{2,1,0:T(8,128)(2,1)S(1)}, bf16[1,256,4096]{2,1,0:T(8,128)(2,1)}, u32[]{:S(2)}) copy-start(bf16[1,256,4096]{2,1,0:T(8,128)(2,1)} %param.6) | copy-start | bytes 6291460
  6.5 41.1 %copy-start.1 = (f32[1,256]{1,0:T(1,128)S(1)}, f32[1,256]{1,0:T(1,128)}, u32[]{:S(2)}) copy-start(f32[1,256]{1,0:T(1,128)} %param.7) | copy-start | bytes 3076
  6.5 60.7 %reduce-scatter.2.cloned.1.call-start = ((), (), s32[]{:S(2)}) async-start(), calls=%async_computation.1 | async-start | bytes 40960 | tf_op jit(solution)/shard_map/reduce_scatter | solution.py:16
Sparse Core Ops, SparseCore 0:
  49.1 18.0 reduce-scatter.1
where the time goes:
time: 74.3 us; the launch traced here: 74.1 us
  blocking collectives  32.1 us (43%)
  waiting for transfers between devices  18.3 us (25%)
  between operations  13.4 us (18%)
  matrix products  10.3 us (14%)
    psum x1, blocking collectives, shards(): projected = lax.psum(partial_sum, 'dp').astype(jnp.bfloat16)  32.1 us
    reduce_scatter x1, waiting for transfers between devices, shards(): lax.psum_scatter(totals, ('feat', 'ens'), scatter_dimension=0, tiled=True)  18.2 us
    dot_general x1, matrix products, shards(): jnp.dot(test_local, inverse_local, preferred_element_type=jnp.float32)  8.96 us
  transfers between devices with their start and end apart: 1, of which 1 were waited for; matrix products, arithmetic and copies ran while one was open for 0% of the time, Pallas kernels for 0%

commit v1 on v0

--- a/solution.py
+++ b/solution.py
@@ -2,6 +2,11 @@
 import jax.numpy as jnp
 from jax import lax
 from jax.sharding import PartitionSpec as P
+
+
+def add_all(x, name):
+    blocks = lax.all_gather(x, name)
+    return jnp.sum(blocks, axis=0)
 
 
 def shards(test_feat, kernel_inverse, train_feat, residual_weight):
@@ -10,7 +15,7 @@
     train_local = train_feat[0]
     weight_row = residual_weight[0][None, :]
     partial_sum = jnp.dot(test_local, inverse_local, preferred_element_type=jnp.float32)
-    projected = lax.psum(partial_sum, "dp").astype(jnp.bfloat16)
+    projected = add_all(partial_sum, "dp").astype(jnp.bfloat16)
     raw = jnp.einsum("tf,nf->tn", projected, train_local, preferred_element_type=jnp.float32)
     totals = raw * weight_row
     return lax.psum_scatter(totals, ("feat", "ens"), scatter_dimension=0, tiled=True)

time: 74.3 us -> 93.5 us (1.26)
  waiting for transfers between devices: 18.3 us -> 67 us
  blocking collectives: 32.1 us -> 0 us
  other arithmetic: 0 us -> 1.75 us
    all_gather x0 -> x1, waiting for transfers between devices: none -> 48.5 us  [add_all(): blocks = lax.all_gather(x, name)]
    psum x1 -> x0, blocking collectives: 32.1 us -> none  [shards(): projected = lax.psum(partial_sum, 'dp').astype(jnp.bfloat16)]
    reduce_sum x0 -> x1, other arithmetic: none -> 1.75 us  [add_all(): return jnp.sum(blocks, axis=0)]
  transfers between devices with their start and end apart: 1 -> 2, of which waited for: 1 -> 2; matrix products, arithmetic and copies ran while one was open for 0% -> 0% of each run, Pallas kernels for 0% -> 0%
where the time goes in v1:
time: 93.5 us; the launch traced here: 93.3 us
  waiting for transfers between devices  67 us (72%)
  between operations  13.4 us (14%)
  matrix products  11.1 us (12%)
  other arithmetic  1.75 us (2%)
    all_gather x1, waiting for transfers between devices, add_all(): blocks = lax.all_gather(x, name)  48.5 us
    reduce_scatter x1, waiting for transfers between devices, shards(): lax.psum_scatter(totals, ('feat', 'ens'), scatter_dimension=0, tiled=True)  18.5 us
    dot_general x1, matrix products, shards(): jnp.dot(test_local, inverse_local, preferred_element_type=jnp.float32)  9.76 us
  transfers between devices with their start and end apart: 2, of which 2 were waited for; matrix products, arithmetic and copies ran while one was open for 0% of the time, Pallas kernels for 0%

profile of v1, /device:TPU:0, one launch (start us, length us, event | category | flops | bytes accessed | tf_op | source)
XLA Modules:
  0.0 93.3 jit_solution(13089435950425511893)
XLA Ops:
  6.5 0.0 copy-start
  6.5 0.0 all-gather.3.cloned.1.call-start
  6.5 9.8 %fusion = f32[32,4096]{1,0:T(8,128)} fusion(bf16[1,2048,4096]{2,1,0:T(8,128)(2,1)} %param.5, bf16[1,32,2048]{2,1,0:T(8,128)(2,1)} %param.4), kind=kOutput, calls=%fused_computation | convolution fusion | flops 536870912 | bytes 17432576 | tf_op jit(solution)/shard_map/dot_general | solution.py:17
  16.3 0.0 copy-start.1
  16.3 0.0 all-gather.3.cloned.1.call-update
  16.3 0.0 reduce-scatter.2.cloned.1.call-start
  16.4 48.5 %all-gather.3.cloned.1.call-done = f32[128,4096]{1,0:T(8,128)} async-done(((f32[32,4096]{1,0:T(8,128)}), f32[128,4096]{1,0:T(8,128)}) %all-gather.3.cloned.1.call-update) | async-done | bytes 2097168 | tf_op jit(solution)/shard_map/all_gather | solution.py:8
  64.9 1.7 %reduce_sum.9 = bf16[32,4096]{1,0:T(8,128)(2,1)S(1)} reduce(f32[4,32,4096]{2,1,0:T(8,128)} %bitcast.14, f32[]{:T(128)} %constant.0.clone.1), dimensions={0}, to_apply=%region_0.0 | reduce | flops 393216 | bytes 2359300 | tf_op jit(solution)/shard_map/reduce_sum | solution.py:9
  66.6 0.0 copy-done
  66.6 0.0 copy-done.1
  66.6 1.4 %fusion.4 = f32[32,256]{1,0:T(8,128)} fusion(bf16[1,256,4096]{2,1,0:T(8,128)(2,1)S(1)} %copy-done, bf16[32,4096]{1,0:T(8,128)(2,1)S(1)} %reduce_sum.9, f32[256]{0:T(256)S(1)} %bitcast.15), kind=kOutput, calls=%fused_computation.4 | convolution fusion | flops 67117056 | bytes 2393088 | tf_op jit(solution)/shard_map/tf,nf->tn/dot_general | solution.py:19
  68.0 0.0 reduce-scatter.2.cloned.1.call-update
  68.0 18.5 %reduce-scatter.2.cloned.1.call-done = f32[8,256]{1,0:T(8,128)} async-done(((f32[32,256]{1,0:T(8,128)}), f32[8,256]{1,0:T(8,128)}) %reduce-scatter.2.cloned.1.call-update) | async-done | bytes 8208 | tf_op jit(solution)/shard_map/reduce_scatter | solution.py:21
Async XLA Ops:
  6.5 60.1 %copy-start = (bf16[1,256,4096]{2,1,0:T(8,128)(2,1)S(1)}, bf16[1,256,4096]{2,1,0:T(8,128)(2,1)}, u32[]{:S(2)}) copy-start(bf16[1,256,4096]{2,1,0:T(8,128)(2,1)} %param.6) | copy-start | bytes 6291460
  6.5 58.3 %all-gather.3.cloned.1.call-start = ((), (), s32[]{:S(2)}) async-start(), calls=%async_computation.2 | async-start | bytes 2621440 | tf_op jit(solution)/shard_map/all_gather | solution.py:8
  16.3 50.3 %copy-start.1 = (f32[1,256]{1,0:T(1,128)S(1)}, f32[1,256]{1,0:T(1,128)}, u32[]{:S(2)}) copy-start(f32[1,256]{1,0:T(1,128)} %param.7) | copy-start | bytes 3076
  16.3 70.2 %reduce-scatter.2.cloned.1.call-start = ((), (), s32[]{:S(2)}) async-start(), calls=%async_computation.1 | async-start | bytes 40960 | tf_op jit(solution)/shard_map/reduce_scatter | solution.py:21
Sparse Core Ops, SparseCore 0:
  16.4 48.3 all-gather.2
  68.1 18.3 reduce-scatter.1
